TPU v7x, 32 devices: a whole 2x2x4 slice. The times are simulated.
32 devices in a mesh: mem: 8 (over y, x, core), reg: 4 (over z).
Axes of the slice: x: 2, y: 2, z: 4, core: 2. Of those that a mesh axis runs over, the one named last changes fastest.
Arguments:
- sample_stack: float32 [64, 11, 8, 256], P('mem', None, 'reg'), may hold values from -6 to 6
- weights: float32 [4, 64], P('reg', 'mem'), may hold values from 0.1 to 10
- offspring: int32 [4, 64], P('reg'), may hold values from 0 to 63
- localize: float32 [8, 256], P('reg'), may hold values from 0.2 to 0.9
Outputs:
- posterior: float32 [64, 11, 8, 256], P('mem', None, 'reg')
Inputs may be any that keep to these rules, and one draw needn't show every extreme that they name: `offspring`: each entry names a member.
All inputs are finite; a program needn't handle non-finite values.
Results may differ from a plain program's by a relative error of at most 0.0021.
Values may be sent and summed in bfloat16 or wider, within the bound.
A program may use at most 64 MiB of HBM per device.

v0:
```python
import jax
import jax.numpy as jnp
from jax import lax
from jax.sharding import PartitionSpec as P

wave_gain = 0.25
advect_gain = 0.1
diffuse_gain = 0.1
small_eps = 1e-05


def extended(block, sides, width):
    for axis, dim in sides:
        count = lax.axis_size(axis)
        forward = [(i, i + 1) for i in range(count - 1)]
        forward.append((count - 1, 0))
        backward = [(target, source) for source, target in forward]
        low = lax.ppermute(
            lax.slice_in_dim(block, block.shape[dim] - width, None, axis=dim), axis, forward
        )
        high = lax.ppermute(lax.slice_in_dim(block, 0, width, axis=dim), axis, backward)
        block = jnp.concatenate([low, block, high], axis=dim)
    return block


def advance(padded):
    centre = padded[:, :, 1:-1]
    upper_rows = padded[:, :, 2:]
    lower_rows = padded[:, :, :-2]
    right_cols = jnp.roll(centre, -1, 3)
    left_cols = jnp.roll(centre, 1, 3)
    slope_east = 0.5 * (right_cols - left_cols)
    slope_north = 0.5 * (upper_rows - lower_rows)
    laplace = right_cols + left_cols + upper_rows + lower_rows - 4.0 * centre
    height = centre[:, 0]
    flow_east = centre[:, 1]
    flow_north = centre[:, 2]
    tracer = centre[:, 3:]
    new_height = height - wave_gain * (slope_east[:, 1] + slope_north[:, 2])
    new_east = flow_east - wave_gain * slope_east[:, 0]
    new_north = flow_north - wave_gain * slope_north[:, 0]
    new_tracer = (
        tracer
        - advect_gain
        * (flow_east[:, None] * slope_east[:, 3:] + flow_north[:, None] * slope_north[:, 3:])
        + diffuse_gain * laplace[:, 3:]
    )
    return jnp.concatenate(
        [new_height[:, None], new_east[:, None], new_north[:, None], new_tracer], axis=1
    )


def single_propagation(model_snapshot):
    padded = extended(model_snapshot, (("reg", 2),), 1)
    return advance(padded)


def per_device(sample_stack, weights, offspring, localize):
    sample_collection = sample_stack.shape[0]
    background_prediction = single_propagation(single_propagation(sample_stack))
    importance_factors = weights[0][:, None, None, None]
    total_local = jnp.sum(weights[0])
    zonal_average_vector = jnp.sum(importance_factors * background_prediction, axis=0)
    weight_total, first_sum = lax.psum((total_local, zonal_average_vector), "mem")
    sample_average_map = first_sum / weight_total
    sample_departure = background_prediction - sample_average_map
    variance = (
        lax.psum(jnp.sum(importance_factors * sample_departure * sample_departure, axis=0), "mem")
        / weight_total
    )
    unrolled_lattice = background_prediction.astype(jnp.bfloat16).reshape(sample_collection, -1)
    source_ids = offspring[0]
    member_base = lax.axis_index("mem") * sample_collection
    own_ids = member_base + jnp.arange(sample_collection, dtype=jnp.int32)
    onehot = (source_ids[:, None] == own_ids[None, :]).astype(jnp.bfloat16)
    sample_duplicates = lax.psum_scatter(
        jnp.dot(onehot, unrolled_lattice, preferred_element_type=jnp.float32).astype(jnp.bfloat16),
        "mem",
        scatter_dimension=0,
        tiled=True,
    ).astype(jnp.float32)
    sample_duplicates = sample_duplicates.reshape(background_prediction.shape)
    cell_weight_value = localize[None, None]
    spread_offset = cell_weight_value * (sample_duplicates - sample_average_map) + (
        1.0 - cell_weight_value
    ) * (background_prediction - sample_average_map)
    total_members = sample_collection * lax.axis_size("mem")
    spread = lax.psum(jnp.sum(spread_offset * spread_offset, axis=0), "mem") / total_members
    scale_ratio = jnp.sqrt((variance + small_eps) / (spread + small_eps))
    return sample_average_map + scale_ratio * spread_offset


def solution(mesh):
    in_specs = (P("mem", None, "reg", None), P("reg", "mem"), P("reg", None), P("reg", None))
    out_specs = P("mem", None, "reg", None)
    return jax.shard_map(
        per_device, mesh=mesh, in_specs=in_specs, out_specs=out_specs, check_vma=False
    )
```

profile of v0, /device:TPU:0, one launch (start us, length us, event | category | flops | bytes accessed | tf_op | source)
XLA Modules:
  0.0 99.8 jit_solution(2924346324299373953)
XLA Ops:
  6.5 0.0 copy-start
  6.5 0.0 reduce-scatter.2.cloned.1.call-start
  6.5 1.2 %fusion.51 = (f32[8,11,1,256]{3,2,1,0:T(1,128)S(1)}, f32[8,11,1,256]{3,2,1,0:T(1,128)S(1)}) fusion(f32[8,11,2,256]{3,2,1,0:T(2,128)} %param.4), kind=kLoop, calls=%fused_computation.102 | loop fusion | bytes 360448 | tf_op jit(solution)/shard_map/slice | solution.py:19
  7.8 5.1 %collective-permute-start = (f32[8,11,1,256]{3,2,1,0:T(1,128)S(1)}, f32[8,11,1,256]{3,2,1,0:T(1,128)S(1)}, u32[]{:S(2)}, u32[]{:S(2)}) collective-permute-start(f32[8,11,1,256]{3,2,1,0:T(1,128)S(1)} %get-tuple-element.33), channel_id=1, source_target_pairs={{1,0},{2,1},{3,2},{0,3},{5,4},{6,5},{7,6},{4,7},{9,8},{10,9},{11,1... | collective-permute-start | bytes 270344 | tf_op jit(solution)/shard_map/ppermute | solution.py:21
  12.9 0.0 collective-permute-start.1
  12.9 1.1 %fusion.50 = (f32[8,11,2,1]{3,2,1,0:T(2,128)S(1)}, f32[8,11,2,1]{3,2,1,0:T(2,128)S(1)}) fusion(f32[8,11,2,256]{3,2,1,0:T(2,128)} %param.4), kind=kLoop, calls=%fused_computation.101 | loop fusion | bytes 2816 | tf_op jit(solution)/shard_map/jit(_roll_static)/slice | solution.py:30
  14.0 0.0 copy-done
  14.0 0.3 fusion.49
  14.2 0.4 fusion.3
  14.6 1.1 %collective-permute-done = f32[8,11,1,256]{3,2,1,0:T(1,128)S(1)} collective-permute-done((f32[8,11,1,256]{3,2,1,0:T(1,128)S(1)}, f32[8,11,1,256]{3,2,1,0:T(1,128)S(1)}, u32[]{:S(2)}, u32[]{:S(2)}) %collective-permute-start) | collective-permute-done | bytes 90144 | tf_op jit(solution)/shard_map/ppermute | solution.py:21
  15.7 3.5 %collective-permute-done.1 = f32[8,11,1,256]{3,2,1,0:T(1,128)S(1)} collective-permute-done((f32[8,11,1,256]{3,2,1,0:T(1,128)S(1)}, f32[8,11,1,256]{3,2,1,0:T(1,128)S(1)}, u32[]{:S(2)}, u32[]{:S(2)}) %collective-permute-start.1) | collective-permute-done | bytes 90144 | tf_op jit(solution)/shard_map/ppermute | solution.py:18
  19.2 0.3 fusion.5
  19.6 0.6 fusion.32
  20.2 0.1 pad_maximum_fusion.14
  20.3 0.1 fusion.48
  20.4 0.2 fusion.47
  20.6 0.3 fusion.46
  20.8 0.1 collective-permute-start.3
  20.9 3.8 %collective-permute-start.2 = (f32[8,11,1,256]{3,2,1,0:T(1,128)S(1)}, f32[8,11,1,256]{3,2,1,0:T(1,128)S(1)}, u32[]{:S(2)}, u32[]{:S(2)}) collective-permute-start(f32[8,11,1,256]{3,2,1,0:T(1,128)S(1)} %get-tuple-element.24), channel_id=1, source_target_pairs={{1,0},{2,1},{3,2},{0,3},{5,4},{6,5},{7,6},{4,7},{9,8},{10,9},{11,1... | collective-permute-start | bytes 270344 | tf_op jit(solution)/shard_map/ppermute | solution.py:21
  24.7 0.4 fusion.1
  25.1 2.1 %collective-permute-done.3 = f32[8,11,1,256]{3,2,1,0:T(1,128)S(1)} collective-permute-done((f32[8,11,1,256]{3,2,1,0:T(1,128)S(1)}, f32[8,11,1,256]{3,2,1,0:T(1,128)S(1)}, u32[]{:S(2)}, u32[]{:S(2)}) %collective-permute-start.3) | collective-permute-done | bytes 90144 | tf_op jit(solution)/shard_map/ppermute | solution.py:18
  27.2 0.0 collective-permute-done.2
  27.2 0.4 subtract_multiply_fusion
  27.6 0.0 copy-start.2
  27.6 0.4 fusion.25
  28.1 0.0 copy-start.3
  28.1 0.2 copy-done.2
  28.3 0.2 multiply_reduce_fusion.1
  28.5 0.1 concatenate.46
  28.6 0.1 copy-done.3
  28.7 0.0 copy-start.1
  28.7 1.2 %convolution_convert_fusion = bf16[64,5632]{1,0:T(8,128)(2,1)} fusion(f32[8,5632]{1,0:T(8,128)S(1)} %concatenate.46, s32[8]{0:T(128)S(1)} %iota_add_fusion, s32[64]{0:T(128)S(1)} %bitcast.21), kind=kOutput, calls=%fused_computation | convolution fusion | flops 6173184 | bytes 901408 | tf_op jit(solution)/shard_map/dot_general | solution.py:77
  30.0 0.0 reduce-scatter.2.cloned.1.call-update
  30.0 0.0 copy-done.1
  30.1 0.6 reduce_sum.39
  30.7 23.4 %all-reduce.1 = (f32[11,2,256]{2,1,0:T(2,128)S(1)}, f32[]{:T(128)}) all-reduce(f32[11,2,256]{2,1,0:T(2,128)S(1)} %get-tuple-element.9, f32[]{:T(128)} %reduce_sum.39), channel_id=1, replica_groups=mesh['mem'=8,'reg'=4] {'mem'}, use_global_device_ids=true, to_apply=%region_1.2 | all-reduce | flops 5633 | bytes 45064 | tf_op jit(solution)/shard_map/psum | solution.py:64
  54.1 0.7 broadcast_divide_fusion
  54.8 0.2 fusion.6
  55.0 11.4 %reduce-scatter.2.cloned.1.call-done = bf16[8,5632]{1,0:T(8,128)(2,1)} async-done(((bf16[64,5632]{1,0:T(8,128)(2,1)}), bf16[8,5632]{1,0:T(8,128)(2,1)}) %reduce-scatter.2.cloned.1.call-update) | async-done | bytes 90128 | tf_op jit(solution)/shard_map/reduce_scatter | solution.py:76
  66.4 0.9 convert
  67.3 1.0 multiply_reduce_fusion
  68.3 23.1 %all-reduce = (f32[11,2,256]{2,1,0:T(2,128)S(1)}, f32[11,2,256]{2,1,0:T(2,128)S(1)}) all-reduce(f32[11,2,256]{2,1,0:T(2,128)S(1)} %reduce_sum.42, f32[11,2,256]{2,1,0:T(2,128)S(1)} %fusion.6), channel_id=1, replica_groups=mesh['mem'=8,'reg'=4] {'mem'}, use_global_device_ids=true, to_apply=%region_8.9 | all-reduce | flops 11264 | bytes 90112 | tf_op jit(solution)/shard_map/psum | solution.py:88
  91.4 0.7 fusion.35
  92.1 0.8 fusion.10
  (10 shorter events, 0.2 us)
Async XLA Ops:
  6.5 7.4 %copy-start = (f32[8,11,2,256]{3,2,1,0:T(2,128)S(1)}, f32[8,11,2,256]{3,2,1,0:T(2,128)}, u32[]{:S(2)}) copy-start(f32[8,11,2,256]{3,2,1,0:T(2,128)} %param.4) | copy-start | bytes 540676
  6.5 59.8 %reduce-scatter.2.cloned.1.call-start = ((), (), s32[]{:S(2)}) async-start(), calls=%async_computation.1 | async-start | bytes 811008 | tf_op jit(solution)/shard_map/reduce_scatter | solution.py:76
  7.8 7.9 %collective-permute-start = (f32[8,11,1,256]{3,2,1,0:T(1,128)S(1)}, f32[8,11,1,256]{3,2,1,0:T(1,128)S(1)}, u32[]{:S(2)}, u32[]{:S(2)}) collective-permute-start(f32[8,11,1,256]{3,2,1,0:T(1,128)S(1)} %get-tuple-element.33), channel_id=1, source_target_pairs={{1,0},{2,1},{3,2},{0,3},{5,4},{6,5},{7,6},{4,7},{9,8},{10,9},{11,1... | collective-permute-start | bytes 270344 | tf_op jit(solution)/shard_map/ppermute | solution.py:21
  12.9 6.3 %collective-permute-start.1 = (f32[8,11,1,256]{3,2,1,0:T(1,128)S(1)}, f32[8,11,1,256]{3,2,1,0:T(1,128)S(1)}, u32[]{:S(2)}, u32[]{:S(2)}) collective-permute-start(f32[8,11,1,256]{3,2,1,0:T(1,128)S(1)} %get-tuple-element.32), channel_id=1, source_target_pairs={{0,1},{1,2},{2,3},{3,0},{4,5},{5,6},{6,7},{7,4},{8,9},{9,10},{10,1... | collective-permute-start | bytes 270344 | tf_op jit(solution)/shard_map/ppermute | solution.py:18
  20.8 6.4 %collective-permute-start.3 = (f32[8,11,1,256]{3,2,1,0:T(1,128)S(1)}, f32[8,11,1,256]{3,2,1,0:T(1,128)S(1)}, u32[]{:S(2)}, u32[]{:S(2)}) collective-permute-start(f32[8,11,1,256]{3,2,1,0:T(1,128)S(1)} %get-tuple-element.25), channel_id=1, source_target_pairs={{0,1},{1,2},{2,3},{3,0},{4,5},{5,6},{6,7},{7,4},{8,9},{9,10},{10,1... | collective-permute-start | bytes 270344 | tf_op jit(solution)/shard_map/ppermute | solution.py:18
  20.9 6.3 %collective-permute-start.2 = (f32[8,11,1,256]{3,2,1,0:T(1,128)S(1)}, f32[8,11,1,256]{3,2,1,0:T(1,128)S(1)}, u32[]{:S(2)}, u32[]{:S(2)}) collective-permute-start(f32[8,11,1,256]{3,2,1,0:T(1,128)S(1)} %get-tuple-element.24), channel_id=1, source_target_pairs={{1,0},{2,1},{3,2},{0,3},{5,4},{6,5},{7,6},{4,7},{9,8},{10,9},{11,1... | collective-permute-start | bytes 270344 | tf_op jit(solution)/shard_map/ppermute | solution.py:21
  27.6 0.7 copy-start.2
  28.1 0.7 copy-start.3
  28.7 1.3 %copy-start.1 = (f32[2,256]{1,0:T(2,128)S(1)}, f32[2,256]{1,0:T(2,128)}, u32[]{:S(2)}) copy-start(f32[2,256]{1,0:T(2,128)} %param.7) | copy-start | bytes 6148
Sparse Core Ops, SparseCore 0:
  30.1 36.2 reduce-scatter.1
where the time goes:
time: 100 us; the launch traced here: 99.8 us
  blocking collectives  46.5 us (46%)
  waiting for transfers between devices  18.1 us (18%)
  between operations  13.6 us (14%)
  starting transfers between devices  8.97 us (9%)
  other arithmetic  7.64 us (8%)
  local copies, waits for them, and re-layouts  3.69 us (4%)
  matrix products  1.24 us (1%)
    psum x1, blocking collectives, per_device(): lax.psum((total_local, zonal_average_vector), 'mem')  23.4 us
    psum x1, blocking collectives, per_device(): lax.psum(jnp.sum(spread_offset * spread_offset, axis=0), 'mem')  23.1 us
    reduce_scatter x1, waiting for transfers between devices, per_device(): lax.psum_scatter(jnp.dot(onehot, unrolled_lattice, preferred_element_type...  11.4 us
    ppermute x2, starting transfers between devices, extended(): lax.ppermute(lax.slice_in_dim(block, 0, width, axis=dim), axis, backward)  8.91 us
    ppermute x2, waiting for transfers between devices, extended(): lax.ppermute(lax.slice_in_dim(block, block.shape[dim] - width, None, axis...  5.62 us
  transfers between devices with their start and end apart: 5, of which 4 were waited for; matrix products, arithmetic and copies ran while one was open for 4% of the time, Pallas kernels for 0%

commit v1 on v0

v1 whole, which is shorter than its diff:
```python
import functools

import jax
import jax.numpy as jnp
from jax import lax
from jax.experimental import pallas as pl
from jax.experimental.pallas import tpu as pltpu
from jax.sharding import PartitionSpec as P

MESH = pl.DeviceIdType.MESH
wave_gain = 0.25
advect_gain = 0.1
diffuse_gain = 0.1
small_eps = 1e-05
LANES = 128


def rolled(block, shift):
    flat = block.reshape(-1, block.shape[-1])
    return pltpu.roll(flat, shift % block.shape[-1], 1).reshape(block.shape)


def advance(state):
    fields, rows, members, width = state.shape
    centre = state[:, 1:-1]
    upper = state[:, 2:]
    lower = state[:, :-2]
    right = rolled(centre, -1)
    left = rolled(centre, 1)
    height, east, north = centre[0], centre[1], centre[2]
    new_height = height - (0.5 * wave_gain) * ((right[1] - left[1]) + (upper[2] - lower[2]))
    new_east = east - (0.5 * wave_gain) * (right[0] - left[0])
    new_north = north - (0.5 * wave_gain) * (upper[0] - lower[0])
    gain_e = (0.5 * advect_gain) * east
    gain_n = (0.5 * advect_gain) * north
    t_right, t_left, t_up, t_low, t_mid = right[3:], left[3:], upper[3:], lower[3:], centre[3:]
    laplace = t_right + t_left + t_up + t_low - 4.0 * t_mid
    new_tracer = (
        t_mid
        - (gain_e[None] * (t_right - t_left) + gain_n[None] * (t_up - t_low))
        + diffuse_gain * laplace
    )
    return jnp.concatenate([new_height[None], new_east[None], new_north[None], new_tracer], axis=0)


def kernel(
    n, regs, per, x_ref, w_ref, off_ref, loc_ref, out_ref,
    own, low, high, sendb, recv, postb, locs,
    halo_send, halo_recv, to_send, to_recv, back_send, back_recv,
):
    fields, rows, members, width = x_ref.shape
    halves = width // LANES
    me = lax.axis_index("mem")
    band = lax.axis_index("reg")
    above = lax.rem(band + 1, regs)
    below = lax.rem(band + regs - 1, regs)

    barrier = pltpu.get_barrier_semaphore()
    for o in range(1, n):
        pl.semaphore_signal(barrier, inc=1, device_id={"mem": lax.rem(me + o, n)}, device_id_type=MESH)
    for target in (above, below):
        pl.semaphore_signal(barrier, inc=1, device_id={"reg": target}, device_id_type=MESH)
    own[...] = x_ref[...].astype(own.dtype)
    pl.semaphore_wait(barrier, n + 1)

    halos = []
    for i, (target, dst) in enumerate(((above, low), (below, high))):
        copy = pltpu.make_async_remote_copy(
            src_ref=own, dst_ref=dst, send_sem=halo_send.at[i], recv_sem=halo_recv.at[i],
            device_id={"reg": target}, device_id_type=MESH,
        )
        copy.start()
        halos.append(copy)

    for r in range(rows):
        for c in range(halves):
            locs[r * halves + c] = loc_ref[r:r + 1, c * LANES:(c + 1) * LANES]
    eye = lax.broadcasted_iota(jnp.int32, (members, members), 0) == lax.broadcasted_iota(
        jnp.int32, (members, members), 1
    )
    column = jnp.sum(jnp.where(eye, jnp.broadcast_to(w_ref[...], (members, members)), 0.0), axis=1, keepdims=True)
    wide = jnp.broadcast_to(column, (members, LANES))
    total_slabs = fields * rows * halves
    for d in range(n):
        sendb[d, per] = wide
    for k in range(total_slabs, n * per):
        sendb[k // per, k % per] = jnp.zeros((members, LANES), jnp.float32)
    everyone = n * members
    pick = (
        lax.broadcasted_iota(jnp.int32, (everyone, everyone), 0)
        == jnp.broadcast_to(off_ref[...], (everyone, everyone))
    ).astype(jnp.float32).astype(jnp.bfloat16)

    for copy in halos:
        copy.wait_recv()
    state = jnp.concatenate(
        [low[...].astype(jnp.float32), x_ref[...], high[...].astype(jnp.float32)], axis=1
    )
    state = advance(advance(state))
    for f in range(fields):
        for r in range(rows):
            for c in range(halves):
                k = (f * rows + r) * halves + c
                sendb[k // per, k % per] = state[f, r, :, c * LANES:(c + 1) * LANES]

    outgoing = []
    for o in range(1, n):
        peer = lax.rem(me + o, n)
        copy = pltpu.make_async_remote_copy(
            src_ref=sendb.at[peer], dst_ref=recv.at[:, me],
            send_sem=to_send.at[o - 1], recv_sem=to_recv.at[o - 1],
            device_id={"mem": peer}, device_id_type=MESH,
        )
        copy.start()
        outgoing.append(copy)
    for s in range(per + 1):
        recv[s, me] = sendb[me, s]
    for copy in outgoing:
        copy.wait_recv()

    weight = recv[per].reshape(everyone, LANES)
    total = jnp.sum(weight, axis=0, keepdims=True)
    for s in range(per):
        cast = recv[s].reshape(everyone, LANES)
        mean = jnp.sum(weight * cast, axis=0, keepdims=True) / total
        departure = cast - mean
        variance = jnp.sum(weight * departure * departure, axis=0, keepdims=True) / total
        copies = lax.dot_general(
            pick, cast.astype(jnp.bfloat16), (((0,), (0,)), ((), ())), preferred_element_type=jnp.float32
        )
        local = locs[lax.rem(me * per + s, rows * halves)]
        deviation = local * (copies - mean) + (1.0 - local) * departure
        spread = jnp.sum(deviation * deviation, axis=0, keepdims=True) / everyone
        ratio = jnp.sqrt((variance + small_eps) / (spread + small_eps))
        postb[:, s] = (mean + ratio * deviation).reshape(n, members, LANES)

    returned = []
    for o in range(1, n):
        peer = lax.rem(me + o, n)
        copy = pltpu.make_async_remote_copy(
            src_ref=postb.at[peer], dst_ref=out_ref.at[me],
            send_sem=back_send.at[o - 1], recv_sem=back_recv.at[o - 1],
            device_id={"mem": peer}, device_id_type=MESH,
        )
        copy.start()
        returned.append(copy)
    for s in range(per):
        out_ref[me, s] = postb[me, s]
    for copy in halos + outgoing:
        copy.wait_send()
    for copy in returned:
        copy.wait()


def solution(mesh):
    n, regs = mesh.shape["mem"], mesh.shape["reg"]

    def per_device(sample_stack, weights, offspring, localize):
        members, fields, rows, width = sample_stack.shape
        slabs = fields * rows * (width // LANES)
        per = -(-slabs // n)
        x = jnp.transpose(sample_stack, (1, 2, 0, 3))
        vmem = pl.BlockSpec(memory_space=pltpu.VMEM)
        sem = pltpu.SemaphoreType.DMA
        out = pl.pallas_call(
            functools.partial(kernel, n, regs, per),
            out_shape=jax.ShapeDtypeStruct((n, per, members, LANES), jnp.float32),
            in_specs=[vmem] * 4,
            out_specs=vmem,
            scratch_shapes=[
                pltpu.VMEM(x.shape, jnp.bfloat16),
                pltpu.VMEM(x.shape, jnp.bfloat16),
                pltpu.VMEM(x.shape, jnp.bfloat16),
                pltpu.VMEM((n, per + 1, members, LANES), jnp.float32),
                pltpu.VMEM((per + 1, n, members, LANES), jnp.float32),
                pltpu.VMEM((n, per, members, LANES), jnp.float32),
                pltpu.VMEM((rows * (width // LANES), 1, LANES), jnp.float32),
                sem((2,)), sem((2,)), sem((n - 1,)), sem((n - 1,)), sem((n - 1,)), sem((n - 1,)),
            ],
            compiler_params=pltpu.CompilerParams(
                collective_id=0, has_side_effects=True, vmem_limit_bytes=32 << 20
            ),
        )(x, weights, offspring, localize)
        out = out.reshape(n * per, members, LANES)[:slabs]
        out = out.reshape(fields, rows, width // LANES, members, LANES)
        return jnp.transpose(out, (3, 0, 1, 2, 4)).reshape(members, fields, rows, width)

    in_specs = (P("mem", None, "reg", None), P("reg", "mem"), P("reg", None), P("reg", None))
    return jax.shard_map(
        per_device, mesh=mesh, in_specs=in_specs, out_specs=P("mem", None, "reg", None), check_vma=False
    )
```

time: 100 us -> 22.1 us (0.22)
  blocking collectives: 46.5 us -> 0 us
  Pallas kernels: 0 us -> 19.3 us
  waiting for transfers between devices: 18.1 us -> 0 us
  between operations: 13.6 us -> 0.05 us
  starting transfers between devices: 8.97 us -> 0 us
  other arithmetic: 7.64 us -> 0 us
  matrix products: 1.24 us -> 0 us
  local copies, waits for them, and re-layouts: 3.69 us -> 2.58 us
    psum x2 -> x0, blocking collectives: 46.5 us -> none  [the longest x1 23.4 us: per_device(): lax.psum((total_local, zonal_average_vector), 'mem')]
    pallas_call x0 -> x1, Pallas kernels: none -> 19.3 us  [per_device(): pl.pallas_call(functools.partial(kernel, n, regs, per), out_shape=jax.Sha...]
    reduce_scatter x1 -> x0, waiting for transfers between devices: 11.4 us -> none  [per_device(): lax.psum_scatter(jnp.dot(onehot, unrolled_lattice, preferred_element_type...]
    ppermute x4 -> x0, starting transfers between devices: 8.97 us -> none  [the longest x2 8.91 us: extended(): lax.ppermute(lax.slice_in_dim(block, 0, width, axis=dim), axis, backward)]
    ppermute x4 -> x0, waiting for transfers between devices: 6.74 us -> none  [the longest x2 5.62 us: extended(): lax.ppermute(lax.slice_in_dim(block, block.shape[dim] - width, None, axis...]
    slice x6 -> x1, local copies, waits for them, and re-layouts: 3.12 us -> 0.01 us  [per_device(): out = out.reshape(n * per, members, LANES)[:slabs]]
    reduce_sum x4 -> x0, other arithmetic: 1.95 us -> none  [the longest x1 0.99 us: per_device(): jnp.sum(spread_offset * spread_offset, axis=0)]
    add x4 -> x0, other arithmetic: 1.84 us -> none  [the longest x2 1 us: advance(): tracer - advect_gain * (flow_east[:, None] * slope_east[:, 3:] + flow_nor...]
  transfers between devices with their start and end apart: 5 -> 0, of which waited for: 4 -> 0; matrix products, arithmetic and copies ran while one was open for 4% -> 0% of each run, Pallas kernels for 0% -> 0%
where the time goes in v1:
time: 22.1 us; the launch traced here: 21.9 us
  Pallas kernels  19.3 us (87%)
  local copies, waits for them, and re-layouts  2.58 us (12%)
    pallas_call x1, Pallas kernels, per_device(): pl.pallas_call(functools.partial(kernel, n, regs, per), out_shape=jax.Sha...  19.3 us
    unnamed x7, local copies, waits for them, and re-layouts  1.6 us
    reshape x1, local copies, waits for them, and re-layouts, per_device(): jnp.transpose(out, (3, 0, 1, 2, 4)).reshape(members, fields, rows, width)  0.88 us

profile of v1, /device:TPU:0, one launch (start us, length us, event | category | flops | bytes accessed | tf_op | source)
XLA Modules:
  0.0 21.9 jit_solution(17497537546642737425)
XLA Ops:
  0.0 0.0 copy-start
  0.0 0.9 %copy.10 = f32[8,11,2,256]{3,0,2,1:T(8,128)S(1)} copy(f32[8,11,2,256]{3,2,1,0:T(2,128)} %param.4) | data formatting | bytes 360448 | tf_op args[0]
  1.0 0.0 copy-start.1
  1.0 0.0 copy-start.2
  1.0 0.0 copy-done
  1.0 0.6 %copy-done.1 = f32[1,8]{1,0:T(1,128)S(1)} copy-done((f32[1,8]{1,0:T(1,128)S(1)}, f32[1,8]{1,0:T(1,128)}, u32[]{:S(2)}) %copy-start.1) | copy-done | bytes 56
  1.6 0.0 copy-done.2
  1.6 19.3 %shard_map.46 = f32[8,6,8,128]{3,2,1,0:T(8,128)S(1)} custom-call(f32[11,2,8,256]{3,2,1,0:T(8,128)S(1)} %bitcast.9, f32[1,8]{1,0:T(1,128)S(1)} %copy-done.1, s32[1,64]{1,0:T(1,128)S(1)} %copy-done.2, f32[2,256]{1,0:T(2,128)S(1)} %copy-done), custom_call_target="tpu_custom_call" | custom-call | tf_op jit(solution)/shard_map/pallas_call | solution.py:165
  21.0 0.1 copy.9
  21.1 0.9 %reshape.11 = f32[8,11,2,256]{3,2,1,0:T(2,128)} reshape(f32[8,11,2,2,128]{4,3,2,1,0:T(2,128)S(1)} %bitcast.11) | data formatting | bytes 360448 | tf_op jit(solution)/shard_map/reshape | solution.py:186
  (1 shorter events, 0.0 us)
Async XLA Ops:
  0.0 1.0 %copy-start = (f32[2,256]{1,0:T(2,128)S(1)}, f32[2,256]{1,0:T(2,128)}, u32[]{:S(2)}) copy-start(f32[2,256]{1,0:T(2,128)} %loc_ref.1) | copy-start | bytes 6148
  1.0 0.7 %copy-start.1 = (f32[1,8]{1,0:T(1,128)S(1)}, f32[1,8]{1,0:T(1,128)}, u32[]{:S(2)}) copy-start(f32[1,8]{1,0:T(1,128)} %w_ref.1) | copy-start | bytes 100
  1.0 0.7 %copy-start.2 = (s32[1,64]{1,0:T(1,128)S(1)}, s32[1,64]{1,0:T(1,128)}, u32[]{:S(2)}) copy-start(s32[1,64]{1,0:T(1,128)} %off_ref.1) | copy-start | bytes 772

commit v2 on v1

v2 whole, which is shorter than its diff:
```python
import functools

import jax
import jax.numpy as jnp
from jax import lax
from jax.experimental import pallas as pl
from jax.experimental.pallas import tpu as pltpu
from jax.sharding import PartitionSpec as P

MESH = pl.DeviceIdType.MESH
wave_gain = 0.25
advect_gain = 0.1
diffuse_gain = 0.1
small_eps = 1e-05
LANES = 128


def rolled(block, shift):
    flat = block.reshape(-1, block.shape[-1])
    return pltpu.roll(flat, shift % block.shape[-1], 1).reshape(block.shape)


def wave(height, east, north):
    mid = slice(1, -1)
    gain = 0.5 * wave_gain
    inner, flow = height[mid], east[mid]
    new_height = inner - gain * ((rolled(flow, -1) - rolled(flow, 1)) + (north[2:] - north[:-2]))
    new_east = flow - gain * (rolled(inner, -1) - rolled(inner, 1))
    new_north = north[mid] - gain * (height[2:] - height[:-2])
    return new_height, new_east, new_north


def carried(tracer, gain_e, gain_n):
    centre, upper, lower = tracer[:, 1:-1], tracer[:, 2:], tracer[:, :-2]
    right, left = rolled(centre, -1), rolled(centre, 1)
    laplace = right + left + upper + lower - 4.0 * centre
    slopes = gain_e[None] * (right - left) + gain_n[None] * (upper - lower)
    return centre - slopes + diffuse_gain * laplace


def kernel(
    n, regs, per, group, x_ref, w_hbm, off_hbm, loc_hbm, out_ref,
    w_ref, off_ref, loc_ref,
    xin, xown, own, low, high, sendb, recv, postb, locs, wbuf, wrecv,
    in_sem, halo_send, halo_recv, w_send, w_recv, to_send, to_recv, back_send, back_recv,
):
    members, fields, rows, width = x_ref.shape
    halves = width // LANES
    block = rows * halves
    me = lax.axis_index("mem")
    band = lax.axis_index("reg")
    above = lax.rem(band + 1, regs)
    below = lax.rem(band + regs - 1, regs)
    peers = [lax.rem(me + o, n) for o in range(1, n)]
    chunks = []
    for p in range(0, per, group):
        q = min(p + group, per)
        chunks.append((p, q, p * n // block, min(q * n // block, fields)))

    loads = []
    for i, (p, q, f, g) in enumerate(chunks):
        copy = pltpu.make_async_copy(x_ref.at[:, f:g], xin.at[:, f:g], in_sem.at[i])
        copy.start()
        loads.append(copy)
    small = []
    for i, (src, dst) in enumerate(((w_hbm, w_ref), (off_hbm, off_ref), (loc_hbm, loc_ref))):
        copy = pltpu.make_async_copy(src, dst, in_sem.at[len(chunks) + i])
        copy.start()
        small.append(copy)
    barrier = pltpu.get_barrier_semaphore()
    for target in (above, below):
        pl.semaphore_signal(barrier, inc=1, device_id={"reg": target}, device_id_type=MESH)
    for peer in peers:
        pl.semaphore_signal(barrier, inc=1, device_id={"mem": peer}, device_id_type=MESH)

    halos = []
    for i, (p, q, f, g) in enumerate(chunks):
        loads[i].wait()
        for k in range(f, g):
            for r in range(rows):
                piece = xin[:, k, r, :]
                xown[k, r] = piece
                own[k, r] = piece.astype(own.dtype)
        if i == 0:
            pl.semaphore_wait(barrier, n + 1)
        pair = []
        for j, (target, dst) in enumerate(((above, low), (below, high))):
            copy = pltpu.make_async_remote_copy(
                src_ref=own.at[f:g], dst_ref=dst.at[f:g],
                send_sem=halo_send.at[2 * i + j], recv_sem=halo_recv.at[2 * i + j],
                device_id={"reg": target}, device_id_type=MESH,
            )
            copy.start()
            pair.append(copy)
        halos.append(pair)

    for copy in small:
        copy.wait()
    eye = lax.broadcasted_iota(jnp.int32, (members, members), 0) == lax.broadcasted_iota(
        jnp.int32, (members, members), 1
    )
    column = jnp.sum(jnp.where(eye, jnp.broadcast_to(w_ref[...], (members, members)), 0.0), axis=1, keepdims=True)
    wide = jnp.broadcast_to(column, (members, LANES))
    wbuf[...] = wide
    shares = []
    for o, peer in enumerate(peers):
        copy = pltpu.make_async_remote_copy(
            src_ref=wbuf, dst_ref=wrecv.at[me], send_sem=w_send.at[o], recv_sem=w_recv.at[o],
            device_id={"mem": peer}, device_id_type=MESH,
        )
        copy.start()
        shares.append(copy)
    wrecv[me] = wide
    for r in range(rows):
        for c in range(halves):
            locs[r * halves + c] = loc_ref[r:r + 1, c * LANES:(c + 1) * LANES]
    slabs = fields * block
    for k in range(slabs, n * per):
        sendb[k % n, k // n] = jnp.zeros((members, LANES), jnp.float32)
    everyone = n * members
    pick = (
        lax.broadcasted_iota(jnp.int32, (everyone, everyone), 0)
        == jnp.broadcast_to(off_ref[...], (everyone, everyone))
    ).astype(jnp.float32).astype(jnp.bfloat16)

    def store(field, value):
        for r in range(rows):
            for c in range(halves):
                k = (field * rows + r) * halves + c
                sendb[k % n, k // n] = value[r, :, c * LANES:(c + 1) * LANES]

    held = {}

    def forecast(i):
        p, q, f, g = chunks[i]
        for copy in halos[i]:
            copy.wait_recv()
        state = jnp.concatenate(
            [low[f:g].astype(jnp.float32), xown[f:g], high[f:g].astype(jnp.float32)], axis=1
        )
        first = 0
        if i == 0:
            height, east, north = state[0], state[1], state[2]
            held["e0"] = (0.5 * advect_gain) * east[1:-1]
            held["n0"] = (0.5 * advect_gain) * north[1:-1]
            height, east, north = wave(height, east, north)
            held["e1"] = (0.5 * advect_gain) * east[1:-1]
            held["n1"] = (0.5 * advect_gain) * north[1:-1]
            for field, value in enumerate(wave(height, east, north)):
                store(field, value)
            first = 3
        tracer = carried(state[first:], held["e0"], held["n0"])
        tracer = carried(tracer, held["e1"], held["n1"])
        for field in range(f + first, g):
            store(field, tracer[field - f - first])
        copies = []
        for o, peer in enumerate(peers):
            slot = i * (n - 1) + o
            copy = pltpu.make_async_remote_copy(
                src_ref=sendb.at[peer, p:q], dst_ref=recv.at[p:q, me],
                send_sem=to_send.at[slot], recv_sem=to_recv.at[slot],
                device_id={"mem": peer}, device_id_type=MESH,
            )
            copy.start()
            copies.append(copy)
        for s in range(p, q):
            recv[s, me] = sendb[me, s]
        return copies

    def analyse(i, arrivals):
        p, q, f, g = chunks[i]
        for copy in arrivals:
            copy.wait_recv()
        if i == 0:
            for copy in shares:
                copy.wait_recv()
            held["w"] = wrecv[...].reshape(everyone, LANES)
            held["total"] = jnp.sum(held["w"], axis=0, keepdims=True)
        weight, total = held["w"], held["total"]
        for s in range(p, q):
            cast = recv[s].reshape(everyone, LANES)
            mean = jnp.sum(weight * cast, axis=0, keepdims=True) / total
            departure = cast - mean
            variance = jnp.sum(weight * departure * departure, axis=0, keepdims=True) / total
            copies = lax.dot_general(
                pick, cast.astype(jnp.bfloat16), (((0,), (0,)), ((), ())), preferred_element_type=jnp.float32
            )
            local = locs[lax.rem(me + s * n, block)]
            deviation = local * (copies - mean) + (1.0 - local) * departure
            spread = jnp.sum(deviation * deviation, axis=0, keepdims=True) / everyone
            ratio = jnp.sqrt((variance + small_eps) / (spread + small_eps))
            postb[:, s] = (mean + ratio * deviation).reshape(n, members, LANES)
        copies = []
        for o, peer in enumerate(peers):
            slot = i * (n - 1) + o
            copy = pltpu.make_async_remote_copy(
                src_ref=postb.at[peer, p:q], dst_ref=out_ref.at[p:q, me],
                send_sem=back_send.at[slot], recv_sem=back_recv.at[slot],
                device_id={"mem": peer}, device_id_type=MESH,
            )
            copy.start()
            copies.append(copy)
        for s in range(p, q):
            out_ref[s, me] = postb[me, s]
        return copies

    sent, returned = [], []
    last = len(chunks) - 1
    for i in range(last + 1):
        sent.append(forecast(i))
        if i >= 1:
            returned.append(analyse(i - 1, sent[i - 1]))
    returned.append(analyse(last, sent[last]))

    for pair in halos:
        for copy in pair:
            copy.wait_send()
    for copy in shares + sum(sent, []):
        copy.wait_send()
    for copy in sum(returned, []):
        copy.wait()


def solution(mesh):
    n, regs = mesh.shape["mem"], mesh.shape["reg"]

    def per_device(sample_stack, weights, offspring, localize):
        members, fields, rows, width = sample_stack.shape
        halves = width // LANES
        slabs = fields * rows * halves
        per = -(-slabs // n)
        group = max(1, 16 // n)
        steps = -(-per // group)
        turned = (fields, rows, members, width)
        vmem = pl.BlockSpec(memory_space=pltpu.VMEM)
        sem = pltpu.SemaphoreType.DMA
        out = pl.pallas_call(
            functools.partial(kernel, n, regs, per, group),
            out_shape=jax.ShapeDtypeStruct((per, n, members, LANES), jnp.float32),
            in_specs=[pl.BlockSpec(memory_space=pltpu.HBM)] * 4,
            out_specs=vmem,
            scratch_shapes=[
                pltpu.VMEM(weights.shape, weights.dtype),
                pltpu.VMEM(offspring.shape, offspring.dtype),
                pltpu.VMEM(localize.shape, localize.dtype),
                pltpu.VMEM(sample_stack.shape, jnp.float32),
                pltpu.VMEM(turned, jnp.float32),
                pltpu.VMEM(turned, jnp.bfloat16),
                pltpu.VMEM(turned, jnp.bfloat16),
                pltpu.VMEM(turned, jnp.bfloat16),
                pltpu.VMEM((n, per, members, LANES), jnp.float32),
                pltpu.VMEM((per, n, members, LANES), jnp.float32),
                pltpu.VMEM((n, per, members, LANES), jnp.float32),
                pltpu.VMEM((rows * halves, 1, LANES), jnp.float32),
                pltpu.VMEM((members, LANES), jnp.float32),
                pltpu.VMEM((n, members, LANES), jnp.float32),
                sem((steps + 3,)), sem((2 * steps,)), sem((2 * steps,)), sem((n - 1,)), sem((n - 1,)),
                sem((steps * (n - 1),)), sem((steps * (n - 1),)), sem((steps * (n - 1),)), sem((steps * (n - 1),)),
            ],
            compiler_params=pltpu.CompilerParams(
                collective_id=0, has_side_effects=True, vmem_limit_bytes=32 << 20
            ),
        )(sample_stack, weights, offspring, localize)
        out = out.reshape(n * per, members, LANES)[:slabs]
        out = out.reshape(fields, rows, halves, members, LANES)
        return jnp.transpose(out, (3, 0, 1, 2, 4)).reshape(members, fields, rows, width)

    in_specs = (P("mem", None, "reg", None), P("reg", "mem"), P("reg", None), P("reg", None))
    return jax.shard_map(
        per_device, mesh=mesh, in_specs=in_specs, out_specs=P("mem", None, "reg", None), check_vma=False
    )
```

time: 22.1 us -> 25 us (1.13)
  Pallas kernels: 19.3 us -> 20.9 us
  local copies, waits for them, and re-layouts: 2.58 us -> 3.9 us
    pallas_call x1, Pallas kernels: 19.3 us -> 20.9 us  [per_device(): pl.pallas_call(functools.partial(kernel, n, regs, per, group), out_shape=...]
    unnamed x7 -> x8, local copies, waits for them, and re-layouts: 1.6 us -> 2.91 us
where the time goes in v2:
time: 25 us; the launch traced here: 24.9 us
  Pallas kernels  20.9 us (84%)
  local copies, waits for them, and re-layouts  3.9 us (16%)
    pallas_call x1, Pallas kernels, per_device(): pl.pallas_call(functools.partial(kernel, n, regs, per, group), out_shape=...  20.9 us
    unnamed x8, local copies, waits for them, and re-layouts  2.91 us
    reshape x1, local copies, waits for them, and re-layouts, per_device(): jnp.transpose(out, (3, 0, 1, 2, 4)).reshape(members, fields, rows, width)  0.88 us

profile of v2, /device:TPU:0, one launch (start us, length us, event | category | flops | bytes accessed | tf_op | source)
XLA Modules:
  0.0 24.9 jit_solution(5939087018656454909)
XLA Ops:
  0.0 0.0 copy-start
  0.0 0.9 %copy-done = f32[8,11,2,256]{3,2,1,0:T(2,128)S(1)} copy-done((f32[8,11,2,256]{3,2,1,0:T(2,128)S(1)}, f32[8,11,2,256]{3,2,1,0:T(2,128)}, u32[]{:S(2)}) %copy-start) | copy-done | bytes 180248
  0.9 0.0 copy-start.1
  0.9 0.7 %copy-done.1 = f32[2,256]{1,0:T(2,128)S(1)} copy-done((f32[2,256]{1,0:T(2,128)S(1)}, f32[2,256]{1,0:T(2,128)}, u32[]{:S(2)}) %copy-start.1) | copy-done | bytes 2072
  1.6 0.0 copy-start.2
  1.6 0.7 %copy-done.2 = f32[1,8]{1,0:T(1,128)S(1)} copy-done((f32[1,8]{1,0:T(1,128)S(1)}, f32[1,8]{1,0:T(1,128)}, u32[]{:S(2)}) %copy-start.2) | copy-done | bytes 56
  2.3 0.0 copy-start.3
  2.3 0.7 %copy-done.3 = s32[1,64]{1,0:T(1,128)S(1)} copy-done((s32[1,64]{1,0:T(1,128)S(1)}, s32[1,64]{1,0:T(1,128)}, u32[]{:S(2)}) %copy-start.3) | copy-done | bytes 280
  2.9 20.9 %shard_map.46 = f32[6,8,8,128]{3,2,1,0:T(8,128)S(1)} custom-call(f32[8,11,2,256]{3,2,1,0:T(2,128)S(1)} %copy-done, f32[1,8]{1,0:T(1,128)S(1)} %copy-done.2, s32[1,64]{1,0:T(1,128)S(1)} %copy-done.3, f32[2,256]{1,0:T(2,128)S(1)} %copy-done.1), custom_call_target="tpu_custom_call" | custom-call | tf_op jit(solution)/shard_map/pallas_call | solution.py:237
  23.9 0.1 copy.7
  24.0 0.9 %reshape.11 = f32[8,11,2,256]{3,2,1,0:T(2,128)} reshape(f32[8,11,2,2,128]{4,3,2,1,0:T(2,128)S(1)} %bitcast.7) | data formatting | bytes 360448 | tf_op jit(solution)/shard_map/reshape | solution.py:266
  (1 shorter events, 0.0 us)
Async XLA Ops:
  0.0 0.9 %copy-start = (f32[8,11,2,256]{3,2,1,0:T(2,128)S(1)}, f32[8,11,2,256]{3,2,1,0:T(2,128)}, u32[]{:S(2)}) copy-start(f32[8,11,2,256]{3,2,1,0:T(2,128)} %x_ref.1) | copy-start | bytes 540676
  0.9 0.7 %copy-start.1 = (f32[2,256]{1,0:T(2,128)S(1)}, f32[2,256]{1,0:T(2,128)}, u32[]{:S(2)}) copy-start(f32[2,256]{1,0:T(2,128)} %loc_hbm.1) | copy-start | bytes 6148
  1.6 0.7 %copy-start.2 = (f32[1,8]{1,0:T(1,128)S(1)}, f32[1,8]{1,0:T(1,128)}, u32[]{:S(2)}) copy-start(f32[1,8]{1,0:T(1,128)} %w_hbm.1) | copy-start | bytes 100
  2.3 0.7 %copy-start.3 = (s32[1,64]{1,0:T(1,128)S(1)}, s32[1,64]{1,0:T(1,128)}, u32[]{:S(2)}) copy-start(s32[1,64]{1,0:T(1,128)} %off_hbm.1) | copy-start | bytes 772

commit v3 on v2

--- a/solution.py
+++ b/solution.py
@@ -41,7 +41,7 @@
 def kernel(
     n, regs, per, group, x_ref, w_hbm, off_hbm, loc_hbm, out_ref,
     w_ref, off_ref, loc_ref,
-    xin, xown, own, low, high, sendb, recv, postb, locs, wbuf, wrecv,
+    xin, xown, own, low, high, sendb, recv, postb, locs, wbuf, wrecv, back,
     in_sem, halo_send, halo_recv, w_send, w_recv, to_send, to_recv, back_send, back_recv,
 ):
     members, fields, rows, width = x_ref.shape
@@ -194,14 +194,14 @@
         for o, peer in enumerate(peers):
             slot = i * (n - 1) + o
             copy = pltpu.make_async_remote_copy(
-                src_ref=postb.at[peer, p:q], dst_ref=out_ref.at[p:q, me],
+                src_ref=postb.at[peer, p:q], dst_ref=back.at[p:q, me],
                 send_sem=back_send.at[slot], recv_sem=back_recv.at[slot],
                 device_id={"mem": peer}, device_id_type=MESH,
             )
             copy.start()
             copies.append(copy)
         for s in range(p, q):
-            out_ref[s, me] = postb[me, s]
+            back[s, me] = postb[me, s]
         return copies
 
     sent, returned = [], []
@@ -219,6 +219,11 @@
         copy.wait_send()
     for copy in sum(returned, []):
         copy.wait()
+    for field in range(fields):
+        for r in range(rows):
+            for c in range(halves):
+                k = (field * rows + r) * halves + c
+                out_ref[:, field, r, c * LANES:(c + 1) * LANES] = back[k // n, k % n]
 
 
 def solution(mesh):
@@ -229,14 +234,14 @@
         halves = width // LANES
         slabs = fields * rows * halves
         per = -(-slabs // n)
-        group = max(1, 16 // n)
+        group = max(1, 48 // n)
         steps = -(-per // group)
         turned = (fields, rows, members, width)
         vmem = pl.BlockSpec(memory_space=pltpu.VMEM)
         sem = pltpu.SemaphoreType.DMA
         out = pl.pallas_call(
             functools.partial(kernel, n, regs, per, group),
-            out_shape=jax.ShapeDtypeStruct((per, n, members, LANES), jnp.float32),
+            out_shape=jax.ShapeDtypeStruct(sample_stack.shape, jnp.float32),
             in_specs=[pl.BlockSpec(memory_space=pltpu.HBM)] * 4,
             out_specs=vmem,
             scratch_shapes=[
@@ -254,16 +259,15 @@
                 pltpu.VMEM((rows * halves, 1, LANES), jnp.float32),
                 pltpu.VMEM((members, LANES), jnp.float32),
                 pltpu.VMEM((n, members, LANES), jnp.float32),
+                pltpu.VMEM((per, n, members, LANES), jnp.float32),
                 sem((steps + 3,)), sem((2 * steps,)), sem((2 * steps,)), sem((n - 1,)), sem((n - 1,)),
                 sem((steps * (n - 1),)), sem((steps * (n - 1),)), sem((steps * (n - 1),)), sem((steps * (n - 1),)),
             ],
             compiler_params=pltpu.CompilerParams(
-                collective_id=0, has_side_effects=True, vmem_limit_bytes=32 << 20
+                collective_id=0, has_side_effects=True, vmem_limit_bytes=60 << 20
             ),
         )(sample_stack, weights, offspring, localize)
-        out = out.reshape(n * per, members, LANES)[:slabs]
-        out = out.reshape(fields, rows, halves, members, LANES)
-        return jnp.transpose(out, (3, 0, 1, 2, 4)).reshape(members, fields, rows, width)
+        return out
 
     in_specs = (P("mem", None, "reg", None), P("reg", "mem"), P("reg", None), P("reg", None))
     return jax.shard_map(

time: 25 us -> 21.9 us (0.88)
  local copies, waits for them, and re-layouts: 3.9 us -> 1.61 us
  Pallas kernels: 20.9 us -> 20.1 us
    unnamed x8 -> x1, local copies, waits for them, and re-layouts: 2.91 us -> 1.61 us
    reshape x2 -> x0, local copies, waits for them, and re-layouts: 0.97 us -> none  [the longest x1 0.88 us: per_device(): jnp.transpose(out, (3, 0, 1, 2, 4)).reshape(members, fields, rows, width)]
    pallas_call x1, Pallas kernels: 20.9 us -> 20.1 us  [per_device(): pl.pallas_call(functools.partial(kernel, n, regs, per, group), out_shape=...]
where the time goes in v3:
time: 21.9 us; the launch traced here: 21.8 us
  Pallas kernels  20.1 us (92%)
  local copies, waits for them, and re-layouts  1.61 us (7%)
    pallas_call x1, Pallas kernels, per_device(): pl.pallas_call(functools.partial(kernel, n, regs, per, group), out_shape=...  20.1 us
    unnamed x1, local copies, waits for them, and re-layouts  1.61 us

profile of v3, /device:TPU:0, one launch (start us, length us, event | category | flops | bytes accessed | tf_op | source)
XLA Modules:
  0.0 21.8 jit_solution(12811569461540489645)
XLA Ops:
  0.0 20.1 %shard_map.46 = f32[8,11,2,256]{3,2,1,0:T(2,128)} custom-call(f32[8,11,2,256]{3,2,1,0:T(2,128)} %x_ref.1, f32[1,8]{1,0:T(1,128)} %w_hbm.1, s32[1,64]{1,0:T(1,128)} %off_hbm.1, f32[2,256]{1,0:T(2,128)} %loc_hbm.1), custom_call_target="tpu_custom_call" | custom-call | tf_op jit(solution)/shard_map/pallas_call | solution.py:242
  20.2 1.6 %copy.6 = f32[8,11,2,256]{3,2,1,0:T(2,128)} copy(f32[8,11,2,256]{3,2,1,0:T(2,128)} %shard_map.46) | data formatting | bytes 360448

commit v4 on v3

--- a/solution.py
+++ b/solution.py
@@ -44,7 +44,7 @@
     xin, xown, own, low, high, sendb, recv, postb, locs, wbuf, wrecv, back,
     in_sem, halo_send, halo_recv, w_send, w_recv, to_send, to_recv, back_send, back_recv,
 ):
-    members, fields, rows, width = x_ref.shape
+    fields, rows, members, width = x_ref.shape
     halves = width // LANES
     block = rows * halves
     me = lax.axis_index("mem")
@@ -57,11 +57,7 @@
         q = min(p + group, per)
         chunks.append((p, q, p * n // block, min(q * n // block, fields)))
 
-    loads = []
-    for i, (p, q, f, g) in enumerate(chunks):
-        copy = pltpu.make_async_copy(x_ref.at[:, f:g], xin.at[:, f:g], in_sem.at[i])
-        copy.start()
-        loads.append(copy)
+    xown = x_ref
     small = []
     for i, (src, dst) in enumerate(((w_hbm, w_ref), (off_hbm, off_ref), (loc_hbm, loc_ref))):
         copy = pltpu.make_async_copy(src, dst, in_sem.at[len(chunks) + i])
@@ -75,12 +71,7 @@
 
     halos = []
     for i, (p, q, f, g) in enumerate(chunks):
-        loads[i].wait()
-        for k in range(f, g):
-            for r in range(rows):
-                piece = xin[:, k, r, :]
-                xown[k, r] = piece
-                own[k, r] = piece.astype(own.dtype)
+        own[f:g] = x_ref[f:g].astype(own.dtype)
         if i == 0:
             pl.semaphore_wait(barrier, n + 1)
         pair = []
@@ -242,7 +233,7 @@
         out = pl.pallas_call(
             functools.partial(kernel, n, regs, per, group),
             out_shape=jax.ShapeDtypeStruct(sample_stack.shape, jnp.float32),
-            in_specs=[pl.BlockSpec(memory_space=pltpu.HBM)] * 4,
+            in_specs=[vmem] + [pl.BlockSpec(memory_space=pltpu.HBM)] * 3,
             out_specs=vmem,
             scratch_shapes=[
                 pltpu.VMEM(weights.shape, weights.dtype),
@@ -264,9 +255,9 @@
                 sem((steps * (n - 1),)), sem((steps * (n - 1),)), sem((steps * (n - 1),)), sem((steps * (n - 1),)),
             ],
             compiler_params=pltpu.CompilerParams(
-                collective_id=0, has_side_effects=True, vmem_limit_bytes=60 << 20
+                collective_id=0, has_side_effects=True, vmem_limit_bytes=32 << 20
             ),
-        )(sample_stack, weights, offspring, localize)
+        )(jnp.transpose(sample_stack, (1, 2, 0, 3)), weights, offspring, localize)
         return out
 
     in_specs = (P("mem", None, "reg", None), P("reg", "mem"), P("reg", None), P("reg", None))

time: 21.9 us -> 21.9 us (level)
  local copies, waits for them, and re-layouts: 1.61 us -> 2.27 us
  Pallas kernels: 20.1 us -> 19.5 us
    unnamed x1 -> x8, local copies, waits for them, and re-layouts: 1.61 us -> 2.27 us
    pallas_call x1, Pallas kernels: 20.1 us -> 19.5 us  [per_device(): pl.pallas_call(functools.partial(kernel, n, regs, per, group), out_shape=...]
where the time goes in v4:
time: 21.9 us; the launch traced here: 21.8 us
  Pallas kernels  19.5 us (89%)
  local copies, waits for them, and re-layouts  2.27 us (10%)
    pallas_call x1, Pallas kernels, per_device(): pl.pallas_call(functools.partial(kernel, n, regs, per, group), out_shape=...  19.5 us
    unnamed x8, local copies, waits for them, and re-layouts  2.27 us

profile of v4, /device:TPU:0, one launch (start us, length us, event | category | flops | bytes accessed | tf_op | source)
XLA Modules:
  0.0 21.8 jit_solution(12049644479425703378)
XLA Ops:
  0.0 0.0 copy-start
  0.0 0.9 %copy.7 = f32[8,11,2,256]{3,0,2,1:T(8,128)S(1)} copy(f32[8,11,2,256]{3,2,1,0:T(2,128)} %param.4) | data formatting | bytes 360448 | tf_op args[0]
  1.0 0.0 copy-start.1
  1.0 0.0 copy-start.2
  1.0 0.0 copy-done
  1.0 0.6 %copy-done.1 = f32[1,8]{1,0:T(1,128)S(1)} copy-done((f32[1,8]{1,0:T(1,128)S(1)}, f32[1,8]{1,0:T(1,128)}, u32[]{:S(2)}) %copy-start.1) | copy-done | bytes 56
  1.6 0.0 copy-done.2
  1.6 19.5 %shard_map.46 = f32[8,11,2,256]{3,2,1,0:T(2,128)S(1)} custom-call(f32[11,2,8,256]{3,2,1,0:T(8,128)S(1)} %bitcast.3, f32[1,8]{1,0:T(1,128)S(1)} %copy-done.1, s32[1,64]{1,0:T(1,128)S(1)} %copy-done.2, f32[2,256]{1,0:T(2,128)S(1)} %copy-done), custom_call_target="tpu_custom_call" | custom-call | tf_op jit(solution)/shard_map/pallas_call | solution.py:233
  21.1 0.7 %copy.9 = f32[8,11,2,256]{3,2,1,0:T(2,128)} copy(f32[8,11,2,256]{3,2,1,0:T(2,128)S(1)} %shard_map.46) | data formatting | bytes 360448
Async XLA Ops:
  0.0 1.0 %copy-start = (f32[2,256]{1,0:T(2,128)S(1)}, f32[2,256]{1,0:T(2,128)}, u32[]{:S(2)}) copy-start(f32[2,256]{1,0:T(2,128)} %loc_hbm.1) | copy-start | bytes 6148
  1.0 0.7 %copy-start.1 = (f32[1,8]{1,0:T(1,128)S(1)}, f32[1,8]{1,0:T(1,128)}, u32[]{:S(2)}) copy-start(f32[1,8]{1,0:T(1,128)} %w_hbm.1) | copy-start | bytes 100
  1.0 0.7 %copy-start.2 = (s32[1,64]{1,0:T(1,128)S(1)}, s32[1,64]{1,0:T(1,128)}, u32[]{:S(2)}) copy-start(s32[1,64]{1,0:T(1,128)} %off_hbm.1) | copy-start | bytes 772
